TPU v7x, 32 devices: a whole 2x2x4 slice. The times are simulated.
32 devices in a mesh: blk: 2 (over y), uly: 16 (over z, x, core).
Axes of the slice: x: 2, y: 2, z: 4, core: 2. Of those that a mesh axis runs over, the one named last changes fastest.
Arguments:
- queries: bfloat16 [4096, 2048], P(('blk', 'uly')), may hold values from -8 to 8
- keys: bfloat16 [4096, 2048], P(('blk', 'uly')), may hold values from -8 to 8
- values: bfloat16 [4096, 2048], P(('blk', 'uly')), may hold values from -6 to 6
- grad_out: bfloat16 [4096, 2048], P(('blk', 'uly')), may hold values from -6 to 6
- doc_start: int32 [32], replicated, may hold values from 0 to 3968, as said below
Outputs:
- grad_queries: bfloat16 [4096, 2048], P(('blk', 'uly'))
- grad_keys: bfloat16 [4096, 2048], P(('blk', 'uly'))
- grad_values: bfloat16 [4096, 2048], P(('blk', 'uly'))
Inputs may be any that keep to these rules, and one draw needn't show every extreme that they name: `doc_start`: each entry is the first position of its block's document, so documents are runs of whole blocks; no document is longer than 8 blocks and one is exactly 8; a document crosses every boundary between groups of 2048 positions and starts at most 7 blocks before it, at one boundary exactly 7; the last block starts a document.
All inputs are finite; a program needn't handle non-finite values.
Results may differ from a plain program's by a relative error of at most 0.0051.
Values may be sent and summed in bfloat16 or wider, within the bound.
A program may use at most 64 MiB of HBM per device.

v0:
```python
import math
import jax
import jax.numpy as jnp
from jax import lax
from jax.sharding import PartitionSpec as P

BLOCK = 128
MAXB = 8


def passed_along(array, axis, by):
    devices = lax.axis_size(axis)
    pairs = [(i, i + by) for i in range(devices) if 0 <= i + by < devices]
    return lax.ppermute(array, axis, pairs)


def body(queries, keys, values, grad_out, doc_start):
    q_all, k_all, v_all, d_all = (
        lax.all_to_all(queries, "uly", split_axis=1, concat_axis=0, tiled=True),
        lax.all_to_all(keys, "uly", split_axis=1, concat_axis=0, tiled=True),
        lax.all_to_all(values, "uly", split_axis=1, concat_axis=0, tiled=True),
        lax.all_to_all(grad_out, "uly", split_axis=1, concat_axis=0, tiled=True),
    )
    group_rows, width = q_all.shape
    tile = 4 * BLOCK
    fetch_rows = (MAXB - 1) * BLOCK
    lead_tiles = -(-fetch_rows // tile)
    lead_rows = lead_tiles * tile
    pad_rows = lead_rows - fetch_rows
    lead_blocks = lead_rows // BLOCK
    local_blocks = group_rows // BLOCK
    ext_rows = lead_rows + group_rows
    group = lax.axis_index("blk")
    scale = 1.0 / math.sqrt(width)
    split_at = group_rows - fetch_rows
    tail_k = k_all[split_at:]
    tail_v = v_all[split_at:]
    far_k, far_v = passed_along((tail_k, tail_v), "blk", 1)
    blank = jnp.zeros((pad_rows, width), jnp.bfloat16)
    ext_k = jnp.concatenate([blank, far_k, k_all], 0)
    ext_v = jnp.concatenate([blank, far_v, v_all], 0)
    padded_docs = jnp.concatenate([jnp.full((lead_blocks,), -1, jnp.int32), doc_start], 0)
    block_doc = lax.dynamic_slice_in_dim(
        padded_docs, group * local_blocks, lead_blocks + local_blocks, 0
    )
    block_doc = jnp.where(jnp.arange(lead_blocks + local_blocks) < pad_rows // BLOCK, -1, block_doc)
    key_doc = jnp.repeat(block_doc, BLOCK)
    first_pos = (group * local_blocks - lead_blocks) * BLOCK
    key_pos = first_pos + jnp.arange(ext_rows, dtype=jnp.int32)
    query_doc = key_doc[lead_rows:]
    query_pos = key_pos[lead_rows:]

    def query_tile(t, carry):
        dq_all, dk_ext, dv_ext, lse_all, delta_all = carry
        q_start = t * tile
        q_rows = lax.dynamic_slice_in_dim(q_all, q_start, tile, 0)
        d_rows = lax.dynamic_slice_in_dim(d_all, q_start, tile, 0)
        q_doc = lax.dynamic_slice_in_dim(query_doc, q_start, tile, 0)
        q_pos = lax.dynamic_slice_in_dim(query_pos, q_start, tile, 0)
        lower = (q_doc[0] - first_pos) // tile
        upper = t + lead_tiles + 1

        def scores(j):
            k_start = j * tile
            k_rows = lax.dynamic_slice_in_dim(ext_k, k_start, tile, 0)
            v_rows = lax.dynamic_slice_in_dim(ext_v, k_start, tile, 0)
            k_doc = lax.dynamic_slice_in_dim(key_doc, k_start, tile, 0)
            k_pos = lax.dynamic_slice_in_dim(key_pos, k_start, tile, 0)
            allowed = (q_doc[:, None] == k_doc[None, :]) & (k_pos[None, :] <= q_pos[:, None])
            score = (
                jnp.einsum("qd,kd->qk", q_rows, k_rows, preferred_element_type=jnp.float32) * scale
            )
            score = jnp.where(allowed, score, -1e30)
            dprob = jnp.einsum("qd,kd->qk", d_rows, v_rows, preferred_element_type=jnp.float32)
            return (k_rows, score, allowed, dprob)

        def first_pass(j, stats):
            top, total, cross = stats
            k_rows, score, allowed, dprob = scores(j)
            new_top = jnp.maximum(top, jnp.max(score, axis=1))
            fade = jnp.exp(top - new_top)
            weight = jnp.where(allowed, jnp.exp(score - new_top[:, None]), 0.0)
            return (
                new_top,
                total * fade + jnp.sum(weight, axis=1),
                cross * fade + jnp.sum(weight * dprob, axis=1),
            )

        start_stats = (
            jnp.full((tile,), -1e30, jnp.float32),
            jnp.zeros((tile,), jnp.float32),
            jnp.zeros((tile,), jnp.float32),
        )
        top, total, cross = lax.fori_loop(lower, upper, first_pass, start_stats)
        lse = top + jnp.log(total)
        delta = cross / total

        def tile_terms(j):
            k_rows, score, allowed, dprob = scores(j)
            prob = jnp.where(allowed, jnp.exp(score - lse[:, None]), 0.0)
            dscore = (prob * (dprob - delta[:, None]) * scale).astype(jnp.bfloat16)
            prob_low = prob.astype(jnp.bfloat16)
            return (k_rows, dscore, prob_low)

        def full_pass(j, acc):
            dq_part, dk_acc, dv_acc = acc
            k_rows, dscore, prob_low = tile_terms(j)
            dq_part = dq_part + jnp.einsum(
                "qk,kd->qd", dscore, k_rows, preferred_element_type=jnp.float32
            )
            k_start = j * tile
            dk_acc = lax.dynamic_update_slice_in_dim(
                dk_acc,
                lax.dynamic_slice_in_dim(dk_acc, k_start, tile, 0)
                + jnp.einsum("qk,qd->kd", dscore, q_rows, preferred_element_type=jnp.float32),
                k_start,
                0,
            )
            dv_acc = lax.dynamic_update_slice_in_dim(
                dv_acc,
                lax.dynamic_slice_in_dim(dv_acc, k_start, tile, 0)
                + jnp.einsum("qk,qd->kd", prob_low, d_rows, preferred_element_type=jnp.float32),
                k_start,
                0,
            )
            return (dq_part, dk_acc, dv_acc)

        start_acc = (jnp.zeros((tile, width), jnp.float32), dk_ext, dv_ext)
        dq_part, dk_ext, dv_ext = lax.fori_loop(lower, upper, full_pass, start_acc)
        dq_all = lax.dynamic_update_slice_in_dim(dq_all, dq_part.astype(jnp.bfloat16), q_start, 0)
        lse_all = lax.dynamic_update_slice_in_dim(lse_all, lse, q_start, 0)
        delta_all = lax.dynamic_update_slice_in_dim(delta_all, delta, q_start, 0)
        return (dq_all, dk_ext, dv_ext, lse_all, delta_all)

    start_carry = (
        jnp.zeros((group_rows, width), jnp.bfloat16),
        jnp.zeros((ext_rows, width), jnp.float32),
        jnp.zeros((ext_rows, width), jnp.float32),
        jnp.zeros((group_rows,), jnp.float32),
        jnp.zeros((group_rows,), jnp.float32),
    )
    dq_all, dk_ext, dv_ext, lse_all, delta_all = lax.fori_loop(
        0, group_rows // tile, query_tile, start_carry
    )
    near_k = dk_ext[pad_rows:lead_rows]
    near_v = dv_ext[pad_rows:lead_rows]
    back_k, back_v = (
        passed_along(near_k.astype(jnp.bfloat16), "blk", -1).astype(near_k.dtype),
        passed_along(near_v.astype(jnp.bfloat16), "blk", -1).astype(near_v.dtype),
    )
    own_k = dk_ext[lead_rows:]
    own_v = dv_ext[lead_rows:]
    own_k = jnp.concatenate([own_k[:split_at], own_k[split_at:] + back_k], 0).astype(jnp.bfloat16)
    own_v = jnp.concatenate([own_v[:split_at], own_v[split_at:] + back_v], 0).astype(jnp.bfloat16)
    grad_q, grad_k, grad_v = (
        lax.all_to_all(dq_all, "uly", split_axis=0, concat_axis=1, tiled=True),
        lax.all_to_all(own_k, "uly", split_axis=0, concat_axis=1, tiled=True),
        lax.all_to_all(own_v, "uly", split_axis=0, concat_axis=1, tiled=True),
    )
    return (grad_q, grad_k, grad_v)


def solution(mesh):
    return jax.shard_map(
        body,
        mesh=mesh,
        in_specs=(
            P(("blk", "uly"), None),
            P(("blk", "uly"), None),
            P(("blk", "uly"), None),
            P(("blk", "uly"), None),
            P(),
        ),
        out_specs=(P(("blk", "uly"), None), P(("blk", "uly"), None), P(("blk", "uly"), None)),
        check_vma=False,
    )
```

profile of v0, /device:TPU:0, one launch (start us, length us, event | category | flops | bytes accessed | tf_op | source)
XLA Modules:
  0.0 212.2 jit_solution(1656074827154237378)
XLA Ops:
  2.6 7.5 %all-to-all-start.2 = ((bf16[128,16,128]{2,0,1:T(8,128)(2,1)}), bf16[128,16,128]{2,0,1:T(8,128)(2,1)S(1)}, u32[]{:S(2)}, u32[]{:S(2)}) async-start(bf16[128,16,128]{2,0,1:T(8,128)(2,1)} %copy_bitcast_fusion.1), calls=%async_computation.2 | async-start | bytes 1048576 | tf_op jit(solution)/shard_map/all_to_all | solution.py:20
  11.1 13.3 %all-to-all-done.2 = bf16[128,16,128]{2,0,1:T(8,128)(2,1)S(1)} async-done(((bf16[128,16,128]{2,0,1:T(8,128)(2,1)}), bf16[128,16,128]{2,0,1:T(8,128)(2,1)S(1)}, u32[]{:S(2)}, u32[]{:S(2)}) %all-to-all-start.2) | async-done | bytes 524320 | tf_op jit(solution)/shard_map/all_to_all | solution.py:20
  24.4 4.2 %all-to-all-start.3 = ((bf16[128,16,128]{2,0,1:T(8,128)(2,1)}), bf16[128,16,128]{2,0,1:T(8,128)(2,1)S(1)}, u32[]{:S(2)}, u32[]{:S(2)}) async-start(bf16[128,16,128]{2,0,1:T(8,128)(2,1)} %copy_bitcast_fusion), calls=%async_computation.3 | async-start | bytes 1048576 | tf_op jit(solution)/shard_map/all_to_all | solution.py:21
  29.5 13.3 %all-to-all-done.3 = bf16[128,16,128]{2,0,1:T(8,128)(2,1)S(1)} async-done(((bf16[128,16,128]{2,0,1:T(8,128)(2,1)}), bf16[128,16,128]{2,0,1:T(8,128)(2,1)S(1)}, u32[]{:S(2)}, u32[]{:S(2)}) %all-to-all-start.3) | async-done | bytes 524320 | tf_op jit(solution)/shard_map/all_to_all | solution.py:21
  42.8 4.2 %all-to-all-start = ((bf16[128,16,128]{2,0,1:T(8,128)(2,1)}), bf16[128,16,128]{2,0,1:T(8,128)(2,1)S(1)}, u32[]{:S(2)}, u32[]{:S(2)}) async-start(bf16[128,16,128]{2,0,1:T(8,128)(2,1)} %copy_bitcast_fusion.3), calls=%async_computation | async-start | bytes 1048576 | tf_op jit(solution)/shard_map/all_to_all | solution.py:19
  48.0 3.4 %collective-permute-start = (bf16[896,128]{1,0:T(8,128)(2,1)S(1)}, bf16[896,128]{1,0:T(8,128)(2,1)S(1)}, u32[]{:S(2)}, u32[]{:S(2)}) collective-permute-start(bf16[896,128]{1,0:T(8,128)(2,1)S(1)} %bitcast.122), channel_id=1, source_target_pairs={{0,16},{1,17},{2,18},{3,19},{4,20},{5,21},{6,22},{7,23},{8,24},{9,... | collective-permute-start | bytes 688136 | tf_op jit(solution)/shard_map/ppermute | solution.py:14
  52.8 8.5 %all-to-all-done = bf16[128,16,128]{2,0,1:T(8,128)(2,1)S(1)} async-done(((bf16[128,16,128]{2,0,1:T(8,128)(2,1)}), bf16[128,16,128]{2,0,1:T(8,128)(2,1)S(1)}, u32[]{:S(2)}, u32[]{:S(2)}) %all-to-all-start) | async-done | bytes 524320 | tf_op jit(solution)/shard_map/all_to_all | solution.py:19
  61.3 4.2 %all-to-all-start.1 = ((bf16[128,16,128]{2,0,1:T(8,128)(2,1)}), bf16[128,16,128]{2,0,1:T(8,128)(2,1)}, u32[]{:S(2)}, u32[]{:S(2)}) async-start(bf16[128,16,128]{2,0,1:T(8,128)(2,1)} %copy_bitcast_fusion.2), calls=%async_computation.1 | async-start | bytes 1048576 | tf_op jit(solution)/shard_map/all_to_all | solution.py:22
  65.8 4.3 %pad_maximum_fusion.1 = (bf16[3072,128]{1,0:T(8,128)(2,1)S(1)}, bf16[3072,128]{1,0:T(8,128)(2,1)}) fusion(bf16[2048,128]{1,0:T(8,128)(2,1)S(1)} %bitcast.116, bf16[896,128]{1,0:T(8,128)(2,1)S(1)} %collective-permute-done.1, bf16[3072]{0:T(1024)(128)(2,1)S(1)} %pad.8.clone, bf16[2048,128]{1,0:T(8,128)(2,1)S(1)} %bitcast.114, ...), kind=kLoop, calls=%fused_computation.48 | loop fusion | flops 4325376 | bytes 3086336 | tf_op jit(solution)/shard_map/concatenate | solution.py:41
  70.1 9.8 %all-to-all-done.1 = bf16[128,16,128]{2,0,1:T(8,128)(2,1)} async-done(((bf16[128,16,128]{2,0,1:T(8,128)(2,1)}), bf16[128,16,128]{2,0,1:T(8,128)(2,1)}, u32[]{:S(2)}, u32[]{:S(2)}) %all-to-all-start.1) | async-done | bytes 524320 | tf_op jit(solution)/shard_map/all_to_all | solution.py:22
  82.1 58.6 %while.115 = (s32[]{:T(128)}, bf16[2048,128]{1,0:T(8,128)(2,1)}, f32[3072,128]{1,0:T(8,128)}, f32[3072,128]{1,0:T(8,128)S(1)}, s32[2048]{0:T(1024)S(1)}, /*index...) while((s32[]{:T(128)}, bf16[2048,128]{1,0:T(8,128)(2,1)}, ...), condition=%wide.region_8.9_spmd.clone.clone, body=%wide.region_0.8_spmd.clone.clone.sunk | while | flops 478156288 | bytes 12199279 | solution.py:142
  84.5 2.3 %while.116 = (s32[]{:T(128)}, f32[512]{0:T(512)S(1)}, f32[512]{0:T(512)S(1)}, f32[512]{0:T(512)S(1)}, s32[]{:T(128)}, /*index=5*/s32[512]{0:T(512)S(1)}, s32[307...) while((s32[]{:T(128)}, f32[512]{0:T(512)S(1)}, ...), condition=%wide.region_5.5_spmd, body=%wide.region_1.4_spmd.sunk | while | flops 139200000 | bytes 3739867 | solution.py:94
  86.8 5.4 %while.117 = (s32[]{:T(128)}, f32[512,128]{1,0:T(8,128)S(1)}, f32[3072,128]{1,0:T(8,128)}, f32[3072,128]{1,0:T(8,128)S(1)}, s32[]{:T(128)}, /*index=5*/s32[512]{...) while((s32[]{:T(128)}, f32[512,128]{1,0:T(8,128)S(1)}, ...), condition=%wide.region_7.7_spmd, body=%wide.region_6.6_spmd.sunk | while | flops 338886656 | bytes 7229687 | solution.py:129
  95.4 4.5 %while.116 = (s32[]{:T(128)}, f32[512]{0:T(512)S(1)}, f32[512]{0:T(512)S(1)}, f32[512]{0:T(512)S(1)}, s32[]{:T(128)}, /*index=5*/s32[512]{0:T(512)S(1)}, s32[307...) while((s32[]{:T(128)}, f32[512]{0:T(512)S(1)}, ...), condition=%wide.region_5.5_spmd, body=%wide.region_1.4_spmd.sunk | while | flops 139200000 | bytes 3739867 | solution.py:94
  100.0 10.8 %while.117 = (s32[]{:T(128)}, f32[512,128]{1,0:T(8,128)S(1)}, f32[3072,128]{1,0:T(8,128)}, f32[3072,128]{1,0:T(8,128)S(1)}, s32[]{:T(128)}, /*index=5*/s32[512]{...) while((s32[]{:T(128)}, f32[512,128]{1,0:T(8,128)S(1)}, ...), condition=%wide.region_7.7_spmd, body=%wide.region_6.6_spmd.sunk | while | flops 338886656 | bytes 7229687 | solution.py:129
  116.1 5.4 %while.117 = (s32[]{:T(128)}, f32[512,128]{1,0:T(8,128)S(1)}, f32[3072,128]{1,0:T(8,128)}, f32[3072,128]{1,0:T(8,128)S(1)}, s32[]{:T(128)}, /*index=5*/s32[512]{...) while((s32[]{:T(128)}, f32[512,128]{1,0:T(8,128)S(1)}, ...), condition=%wide.region_7.7_spmd, body=%wide.region_6.6_spmd.sunk | while | flops 338886656 | bytes 7229687 | solution.py:129
  124.6 4.5 %while.116 = (s32[]{:T(128)}, f32[512]{0:T(512)S(1)}, f32[512]{0:T(512)S(1)}, f32[512]{0:T(512)S(1)}, s32[]{:T(128)}, /*index=5*/s32[512]{0:T(512)S(1)}, s32[307...) while((s32[]{:T(128)}, f32[512]{0:T(512)S(1)}, ...), condition=%wide.region_5.5_spmd, body=%wide.region_1.4_spmd.sunk | while | flops 139200000 | bytes 3739867 | solution.py:94
  129.2 10.8 %while.117 = (s32[]{:T(128)}, f32[512,128]{1,0:T(8,128)S(1)}, f32[3072,128]{1,0:T(8,128)}, f32[3072,128]{1,0:T(8,128)S(1)}, s32[]{:T(128)}, /*index=5*/s32[512]{...) while((s32[]{:T(128)}, f32[512,128]{1,0:T(8,128)S(1)}, ...), condition=%wide.region_7.7_spmd, body=%wide.region_6.6_spmd.sunk | while | flops 338886656 | bytes 7229687 | solution.py:129
  140.7 4.2 %all-to-all-start.4 = ((bf16[16,128,128]{2,1,0:T(8,128)(2,1)}), bf16[16,128,128]{2,1,0:T(8,128)(2,1)S(1)}, u32[]{:S(2)}, u32[]{:S(2)}) async-start(bf16[16,128,128]{2,1,0:T(8,128)(2,1)} %bitcast.118), calls=%async_computation.4 | async-start | bytes 1048576 | tf_op jit(solution)/shard_map/all_to_all | solution.py:156
  146.3 22.9 %collective-permute-done.3 = bf16[896,128]{1,0:T(8,128)(2,1)S(1)} collective-permute-done((bf16[896,128]{1,0:T(8,128)(2,1)S(1)}, bf16[896,128]{1,0:T(8,128)(2,1)S(1)}, u32[]{:S(2)}, u32[]{:S(2)}) %collective-permute-start.3) | collective-permute-done | bytes 229408 | tf_op jit(solution)/shard_map/ppermute | solution.py:14
  170.1 5.7 %all-to-all-start.6 = ((bf16[16,128,128]{2,1,0:T(8,128)(2,1)}), bf16[16,128,128]{2,1,0:T(8,128)(2,1)S(1)}, u32[]{:S(2)}, u32[]{:S(2)}) async-start(bf16[16,128,128]{2,1,0:T(8,128)(2,1)} %bitcast.21), calls=%async_computation.6 | async-start | bytes 1048576 | tf_op jit(solution)/shard_map/all_to_all | solution.py:158
  178.6 10.4 %collective-permute-done.2 = bf16[896,128]{1,0:T(8,128)(2,1)S(1)} collective-permute-done((bf16[896,128]{1,0:T(8,128)(2,1)S(1)}, bf16[896,128]{1,0:T(8,128)(2,1)S(1)}, u32[]{:S(2)}, u32[]{:S(2)}) %collective-permute-start.2) | collective-permute-done | bytes 229408 | tf_op jit(solution)/shard_map/ppermute | solution.py:14
  190.9 5.7 %all-to-all-start.5 = ((bf16[16,128,128]{2,1,0:T(8,128)(2,1)}), bf16[16,128,128]{2,1,0:T(8,128)(2,1)S(1)}, u32[]{:S(2)}, u32[]{:S(2)}) async-start(bf16[16,128,128]{2,1,0:T(8,128)(2,1)} %bitcast.18), calls=%async_computation.5 | async-start | bytes 1048576 | tf_op jit(solution)/shard_map/all_to_all | solution.py:157
  199.2 11.7 %all-to-all-done.5 = bf16[16,128,128]{2,1,0:T(8,128)(2,1)S(1)} async-done(((bf16[16,128,128]{2,1,0:T(8,128)(2,1)}), bf16[16,128,128]{2,1,0:T(8,128)(2,1)S(1)}, u32[]{:S(2)}, u32[]{:S(2)}) %all-to-all-start.5) | async-done | bytes 524320 | tf_op jit(solution)/shard_map/all_to_all | solution.py:157
  (189 shorter events, 76.8 us)
Async XLA Ops:
  0.6 1.0 copy-start
  0.6 9.5 %copy-start.2 = (bf16[128,2048]{1,0:T(8,128)(2,1)S(1)}, bf16[128,2048]{1,0:T(8,128)(2,1)}, u32[]{:S(2)}) copy-start(bf16[128,2048]{1,0:T(8,128)(2,1)} %param.13) | copy-start | bytes 1572868
  2.6 26.0 %copy-start.3 = (bf16[128,2048]{1,0:T(8,128)(2,1)S(1)}, bf16[128,2048]{1,0:T(8,128)(2,1)}, u32[]{:S(2)}) copy-start(bf16[128,2048]{1,0:T(8,128)(2,1)} %param.11) | copy-start | bytes 1572868
  2.6 21.8 %all-to-all-start.2 = ((bf16[128,16,128]{2,0,1:T(8,128)(2,1)}), bf16[128,16,128]{2,0,1:T(8,128)(2,1)S(1)}, u32[]{:S(2)}, u32[]{:S(2)}) async-start(bf16[128,16,128]{2,0,1:T(8,128)(2,1)} %copy_bitcast_fusion.1), calls=%async_computation.2 | async-start | bytes 1048576 | tf_op jit(solution)/shard_map/all_to_all | solution.py:20
  11.1 36.0 %copy-start.4 = (bf16[128,2048]{1,0:T(8,128)(2,1)S(1)}, bf16[128,2048]{1,0:T(8,128)(2,1)}, u32[]{:S(2)}) copy-start(bf16[128,2048]{1,0:T(8,128)(2,1)} %param.14) | copy-start | bytes 1572868
  24.4 18.4 %all-to-all-start.3 = ((bf16[128,16,128]{2,0,1:T(8,128)(2,1)}), bf16[128,16,128]{2,0,1:T(8,128)(2,1)S(1)}, u32[]{:S(2)}, u32[]{:S(2)}) async-start(bf16[128,16,128]{2,0,1:T(8,128)(2,1)} %copy_bitcast_fusion), calls=%async_computation.3 | async-start | bytes 1048576 | tf_op jit(solution)/shard_map/all_to_all | solution.py:21
  42.8 18.4 %all-to-all-start = ((bf16[128,16,128]{2,0,1:T(8,128)(2,1)}), bf16[128,16,128]{2,0,1:T(8,128)(2,1)S(1)}, u32[]{:S(2)}, u32[]{:S(2)}) async-start(bf16[128,16,128]{2,0,1:T(8,128)(2,1)} %copy_bitcast_fusion.3), calls=%async_computation | async-start | bytes 1048576 | tf_op jit(solution)/shard_map/all_to_all | solution.py:19
  47.0 18.5 %copy-start.5 = (s32[32]{0:T(128)S(1)}, s32[32]{0:T(128)}, u32[]{:S(2)}) copy-start(s32[32]{0:T(128)} %param.15) | copy-start | bytes 388
  48.0 17.8 %collective-permute-start = (bf16[896,128]{1,0:T(8,128)(2,1)S(1)}, bf16[896,128]{1,0:T(8,128)(2,1)S(1)}, u32[]{:S(2)}, u32[]{:S(2)}) collective-permute-start(bf16[896,128]{1,0:T(8,128)(2,1)S(1)} %bitcast.122), channel_id=1, source_target_pairs={{0,16},{1,17},{2,18},{3,19},{4,20},{5,21},{6,22},{7,23},{8,24},{9,... | collective-permute-start | bytes 688136 | tf_op jit(solution)/shard_map/ppermute | solution.py:14
  51.5 14.3 %collective-permute-start.1 = (bf16[896,128]{1,0:T(8,128)(2,1)S(1)}, bf16[896,128]{1,0:T(8,128)(2,1)S(1)}, u32[]{:S(2)}, u32[]{:S(2)}) collective-permute-start(bf16[896,128]{1,0:T(8,128)(2,1)S(1)} %bitcast.123), channel_id=1, source_target_pairs={{0,16},{1,17},{2,18},{3,19},{4,20},{5,21},{6,22},{7,23},{8,24},{9,... | collective-permute-start | bytes 688136 | tf_op jit(solution)/shard_map/ppermute | solution.py:14
  61.3 8.8 %copy-start.1 = (bf16[128,16,128]{2,0,1:T(8,128)(2,1)}, bf16[128,16,128]{2,0,1:T(8,128)(2,1)S(1)}, u32[]{:S(2)}) copy-start(bf16[128,16,128]{2,0,1:T(8,128)(2,1)S(1)} %all-to-all-done) | copy-start | bytes 1572868
  61.3 18.5 %all-to-all-start.1 = ((bf16[128,16,128]{2,0,1:T(8,128)(2,1)}), bf16[128,16,128]{2,0,1:T(8,128)(2,1)}, u32[]{:S(2)}, u32[]{:S(2)}) async-start(bf16[128,16,128]{2,0,1:T(8,128)(2,1)} %copy_bitcast_fusion.2), calls=%async_computation.1 | async-start | bytes 1048576 | tf_op jit(solution)/shard_map/all_to_all | solution.py:22
  140.7 29.4 %all-to-all-start.4 = ((bf16[16,128,128]{2,1,0:T(8,128)(2,1)}), bf16[16,128,128]{2,1,0:T(8,128)(2,1)S(1)}, u32[]{:S(2)}, u32[]{:S(2)}) async-start(bf16[16,128,128]{2,1,0:T(8,128)(2,1)} %bitcast.118), calls=%async_computation.4 | async-start | bytes 1048576 | tf_op jit(solution)/shard_map/all_to_all | solution.py:156
  144.9 24.2 %collective-permute-start.3 = (bf16[896,128]{1,0:T(8,128)(2,1)S(1)}, bf16[896,128]{1,0:T(8,128)(2,1)S(1)}, u32[]{:S(2)}, u32[]{:S(2)}) collective-permute-start(bf16[896,128]{1,0:T(8,128)(2,1)S(1)} %slice.80), channel_id=1, source_target_pairs={{16,0},{17,1},{18,2},{19,3},{20,4},{21,5},{22,6},{23,7},{24,8},{25... | collective-permute-start | bytes 688136 | tf_op jit(solution)/shard_map/ppermute | solution.py:14
  170.1 20.9 %all-to-all-start.6 = ((bf16[16,128,128]{2,1,0:T(8,128)(2,1)}), bf16[16,128,128]{2,1,0:T(8,128)(2,1)S(1)}, u32[]{:S(2)}, u32[]{:S(2)}) async-start(bf16[16,128,128]{2,1,0:T(8,128)(2,1)} %bitcast.21), calls=%async_computation.6 | async-start | bytes 1048576 | tf_op jit(solution)/shard_map/all_to_all | solution.py:158
  177.3 11.7 %collective-permute-start.2 = (bf16[896,128]{1,0:T(8,128)(2,1)S(1)}, bf16[896,128]{1,0:T(8,128)(2,1)S(1)}, u32[]{:S(2)}, u32[]{:S(2)}) collective-permute-start(bf16[896,128]{1,0:T(8,128)(2,1)S(1)} %slice.78), channel_id=1, source_target_pairs={{16,0},{17,1},{18,2},{19,3},{20,4},{21,5},{22,6},{23,7},{24,8},{25... | collective-permute-start | bytes 688136 | tf_op jit(solution)/shard_map/ppermute | solution.py:14
  190.9 20.0 %all-to-all-start.5 = ((bf16[16,128,128]{2,1,0:T(8,128)(2,1)}), bf16[16,128,128]{2,1,0:T(8,128)(2,1)S(1)}, u32[]{:S(2)}, u32[]{:S(2)}) async-start(bf16[16,128,128]{2,1,0:T(8,128)(2,1)} %bitcast.18), calls=%async_computation.5 | async-start | bytes 1048576 | tf_op jit(solution)/shard_map/all_to_all | solution.py:157
where the time goes:
time: 214 us; the launch traced here: 212 us
  waiting for transfers between devices  89.9 us (42%)
  starting transfers between devices  43 us (20%)
  matrix products  41.5 us (19%)
  local copies, waits for them, and re-layouts  20 us (9%)
  other arithmetic  13.4 us (6%)
  loops' own time  3.49 us (2%)
    ppermute x4, waiting for transfers between devices, passed_along(): return lax.ppermute(array, axis, pairs)  33.3 us
    dot_general x12, matrix products, scores(): jnp.einsum('qd,kd->qk', q_rows, k_rows, preferred_element_type=jnp.float32)  15.9 us
    all_to_all x1, waiting for transfers between devices, body(): lax.all_to_all(values, 'uly', split_axis=1, concat_axis=0, tiled=True)  13.3 us
    all_to_all x1, waiting for transfers between devices, body(): lax.all_to_all(keys, 'uly', split_axis=1, concat_axis=0, tiled=True)  13.3 us
    dot_general x6, matrix products, full_pass(): jnp.einsum('qk,qd->kd', dscore, q_rows, preferred_element_type=jnp.float32)  11.7 us
    all_to_all x1, waiting for transfers between devices, body(): lax.all_to_all(own_k, 'uly', split_axis=0, concat_axis=1, tiled=True)  11.7 us
    all_to_all x1, waiting for transfers between devices, body(): lax.all_to_all(grad_out, 'uly', split_axis=1, concat_axis=0, tiled=True)  9.77 us
    all_to_all x1, waiting for transfers between devices, body(): lax.all_to_all(queries, 'uly', split_axis=1, concat_axis=0, tiled=True)  8.5 us
  transfers between devices with their start and end apart: 11, of which 7 were waited for; matrix products, arithmetic and copies ran while one was open for 7% of the time, Pallas kernels for 0%

commit v1 on v0

--- a/solution.py
+++ b/solution.py
@@ -17,7 +17,10 @@
 def body(queries, keys, values, grad_out, doc_start):
     q_all, k_all, v_all, d_all = (
         lax.all_to_all(queries, "uly", split_axis=1, concat_axis=0, tiled=True),
-        lax.all_to_all(keys, "uly", split_axis=1, concat_axis=0, tiled=True),
+        jnp.concatenate(
+            lax.all_to_all(jnp.stack(jnp.split(keys, lax.axis_size("uly"), axis=1)), "uly", 0, 0),
+            axis=0,
+        ),
         lax.all_to_all(values, "uly", split_axis=1, concat_axis=0, tiled=True),
         lax.all_to_all(grad_out, "uly", split_axis=1, concat_axis=0, tiled=True),
     )

time: 214 us -> 214 us (level)
  local copies, waits for them, and re-layouts: 20 us -> 29 us
  waiting for transfers between devices: 89.9 us -> 80.9 us
    unnamed x15 -> x30, local copies, waits for them, and re-layouts: 4.09 us -> 13.5 us
    all_to_all x1, waiting for transfers between devices: 13.3 us -> 4.26 us  [body(): lax.all_to_all(values, 'uly', split_axis=1, concat_axis=0, tiled=True)]
    all_to_all x1, starting transfers between devices: 7.52 us -> 4.16 us  [body(): lax.all_to_all(jnp.stack(jnp.split(keys, lax.axis_size('uly'), axis=1)),...]
    all_to_all x1, starting transfers between devices: 4.16 us -> 7.52 us  [body(): lax.all_to_all(values, 'uly', split_axis=1, concat_axis=0, tiled=True)]
  transfers between devices with their start and end apart: 11 -> 11, of which waited for: 7 -> 7; matrix products, arithmetic and copies ran while one was open for 7% -> 11% of each run, Pallas kernels for 0% -> 0%
where the time goes in v1:
time: 214 us; the launch traced here: 212 us
  waiting for transfers between devices  80.9 us (38%)
  starting transfers between devices  43 us (20%)
  matrix products  41.5 us (19%)
  local copies, waits for them, and re-layouts  29 us (14%)
  other arithmetic  13.4 us (6%)
  loops' own time  3.49 us (2%)
    ppermute x4, waiting for transfers between devices, passed_along(): return lax.ppermute(array, axis, pairs)  33.3 us
    dot_general x12, matrix products, scores(): jnp.einsum('qd,kd->qk', q_rows, k_rows, preferred_element_type=jnp.float32)  15.9 us
    unnamed x30, local copies, waits for them, and re-layouts  13.5 us
    all_to_all x1, waiting for transfers between devices, body(): lax.all_to_all(jnp.stack(jnp.split(keys, lax.axis_size('uly'), axis=1)),...  13.3 us
    dot_general x6, matrix products, full_pass(): jnp.einsum('qk,qd->kd', dscore, q_rows, preferred_element_type=jnp.float32)  11.7 us
    all_to_all x1, waiting for transfers between devices, body(): lax.all_to_all(own_k, 'uly', split_axis=0, concat_axis=1, tiled=True)  11.7 us
    all_to_all x1, waiting for transfers between devices, body(): lax.all_to_all(grad_out, 'uly', split_axis=1, concat_axis=0, tiled=True)  9.77 us
    all_to_all x1, waiting for transfers between devices, body(): lax.all_to_all(queries, 'uly', split_axis=1, concat_axis=0, tiled=True)  8.5 us
  transfers between devices with their start and end apart: 11, of which 7 were waited for; matrix products, arithmetic and copies ran while one was open for 11% of the time, Pallas kernels for 0%

profile of v1, /device:TPU:0, one launch (start us, length us, event | category | flops | bytes accessed | tf_op | source)
XLA Modules:
  0.0 212.2 jit_solution(16917816599556105300)
XLA Ops:
  2.6 7.5 %all-to-all-start.3 = ((bf16[128,16,128]{2,0,1:T(8,128)(2,1)}), bf16[128,16,128]{2,0,1:T(8,128)(2,1)S(1)}, u32[]{:S(2)}, u32[]{:S(2)}) async-start(bf16[128,16,128]{2,0,1:T(8,128)(2,1)} %copy_bitcast_fusion), calls=%async_computation.3 | async-start | bytes 1048576 | tf_op jit(solution)/shard_map/all_to_all | solution.py:24
  20.1 4.3 %all-to-all-done.3 = bf16[128,16,128]{2,0,1:T(8,128)(2,1)S(1)} async-done(((bf16[128,16,128]{2,0,1:T(8,128)(2,1)}), bf16[128,16,128]{2,0,1:T(8,128)(2,1)S(1)}, u32[]{:S(2)}, u32[]{:S(2)}) %all-to-all-start.3) | async-done | bytes 524320 | tf_op jit(solution)/shard_map/all_to_all | solution.py:24
  24.4 4.2 %all-to-all-start.2 = ((bf16[16,128,128]{2,1,0:T(8,128)(2,1)}), bf16[16,128,128]{2,1,0:T(8,128)(2,1)S(1)}, u32[]{:S(2)}, u32[]{:S(2)}) async-start(bf16[16,128,128]{2,1,0:T(8,128)(2,1)} %constant_dynamic-update-slice_fusion), calls=%async_computation.2 | async-start | bytes 1048576 | tf_op jit(solution)/shard_map/all_to_all | solution.py:21
  29.5 13.3 %all-to-all-done.2 = bf16[16,128,128]{2,1,0:T(8,128)(2,1)S(1)} async-done(((bf16[16,128,128]{2,1,0:T(8,128)(2,1)}), bf16[16,128,128]{2,1,0:T(8,128)(2,1)S(1)}, u32[]{:S(2)}, u32[]{:S(2)}) %all-to-all-start.2) | async-done | bytes 524320 | tf_op jit(solution)/shard_map/all_to_all | solution.py:21
  42.8 4.2 %all-to-all-start = ((bf16[128,16,128]{2,0,1:T(8,128)(2,1)}), bf16[128,16,128]{2,0,1:T(8,128)(2,1)S(1)}, u32[]{:S(2)}, u32[]{:S(2)}) async-start(bf16[128,16,128]{2,0,1:T(8,128)(2,1)} %copy_bitcast_fusion.2), calls=%async_computation | async-start | bytes 1048576 | tf_op jit(solution)/shard_map/all_to_all | solution.py:19
  48.0 3.4 %collective-permute-start.1 = (bf16[896,128]{1,0:T(8,128)(2,1)S(1)}, bf16[896,128]{1,0:T(8,128)(2,1)S(1)}, u32[]{:S(2)}, u32[]{:S(2)}) collective-permute-start(bf16[896,128]{1,0:T(8,128)(2,1)S(1)} %bitcast.146), channel_id=1, source_target_pairs={{0,16},{1,17},{2,18},{3,19},{4,20},{5,21},{6,22},{7,23},{8,24},{9,... | collective-permute-start | bytes 688136 | tf_op jit(solution)/shard_map/ppermute | solution.py:14
  52.8 8.5 %all-to-all-done = bf16[128,16,128]{2,0,1:T(8,128)(2,1)S(1)} async-done(((bf16[128,16,128]{2,0,1:T(8,128)(2,1)}), bf16[128,16,128]{2,0,1:T(8,128)(2,1)S(1)}, u32[]{:S(2)}, u32[]{:S(2)}) %all-to-all-start) | async-done | bytes 524320 | tf_op jit(solution)/shard_map/all_to_all | solution.py:19
  61.3 4.2 %all-to-all-start.1 = ((bf16[128,16,128]{2,0,1:T(8,128)(2,1)}), bf16[128,16,128]{2,0,1:T(8,128)(2,1)}, u32[]{:S(2)}, u32[]{:S(2)}) async-start(bf16[128,16,128]{2,0,1:T(8,128)(2,1)} %copy_bitcast_fusion.1), calls=%async_computation.1 | async-start | bytes 1048576 | tf_op jit(solution)/shard_map/all_to_all | solution.py:25
  65.8 4.3 %pad_maximum_fusion.1 = (bf16[3072,128]{1,0:T(8,128)(2,1)S(1)}, bf16[3072,128]{1,0:T(8,128)(2,1)}) fusion(bf16[2048,128]{1,0:T(8,128)(2,1)S(1)} %bitcast.139, bf16[896,128]{1,0:T(8,128)(2,1)S(1)} %collective-permute-done.1, bf16[3072]{0:T(1024)(128)(2,1)S(1)} %pad.8.clone, bf16[2048,128]{1,0:T(8,128)(2,1)S(1)} %bitcast.140, ...), kind=kLoop, calls=%fused_computation.48 | loop fusion | flops 4325376 | bytes 3086336 | tf_op jit(solution)/shard_map/concatenate | solution.py:44
  70.1 9.8 %all-to-all-done.1 = bf16[128,16,128]{2,0,1:T(8,128)(2,1)} async-done(((bf16[128,16,128]{2,0,1:T(8,128)(2,1)}), bf16[128,16,128]{2,0,1:T(8,128)(2,1)}, u32[]{:S(2)}, u32[]{:S(2)}) %all-to-all-start.1) | async-done | bytes 524320 | tf_op jit(solution)/shard_map/all_to_all | solution.py:25
  82.1 58.6 %while.115 = (s32[]{:T(128)}, bf16[2048,128]{1,0:T(8,128)(2,1)}, f32[3072,128]{1,0:T(8,128)}, f32[3072,128]{1,0:T(8,128)S(1)}, s32[2048]{0:T(1024)S(1)}, /*index...) while((s32[]{:T(128)}, bf16[2048,128]{1,0:T(8,128)(2,1)}, ...), condition=%wide.region_8.9_spmd.clone.clone, body=%wide.region_0.8_spmd.clone.clone.sunk | while | flops 478156288 | bytes 12199279 | solution.py:145
  84.5 2.3 %while.116 = (s32[]{:T(128)}, f32[512]{0:T(512)S(1)}, f32[512]{0:T(512)S(1)}, f32[512]{0:T(512)S(1)}, s32[]{:T(128)}, /*index=5*/s32[512]{0:T(512)S(1)}, s32[307...) while((s32[]{:T(128)}, f32[512]{0:T(512)S(1)}, ...), condition=%wide.region_5.5_spmd, body=%wide.region_1.4_spmd.sunk | while | flops 139200000 | bytes 3739867 | solution.py:97
  86.8 5.4 %while.117 = (s32[]{:T(128)}, f32[512,128]{1,0:T(8,128)S(1)}, f32[3072,128]{1,0:T(8,128)}, f32[3072,128]{1,0:T(8,128)S(1)}, s32[]{:T(128)}, /*index=5*/s32[512]{...) while((s32[]{:T(128)}, f32[512,128]{1,0:T(8,128)S(1)}, ...), condition=%wide.region_7.7_spmd, body=%wide.region_6.6_spmd.sunk | while | flops 338886656 | bytes 7229687 | solution.py:132
  95.4 4.5 %while.116 = (s32[]{:T(128)}, f32[512]{0:T(512)S(1)}, f32[512]{0:T(512)S(1)}, f32[512]{0:T(512)S(1)}, s32[]{:T(128)}, /*index=5*/s32[512]{0:T(512)S(1)}, s32[307...) while((s32[]{:T(128)}, f32[512]{0:T(512)S(1)}, ...), condition=%wide.region_5.5_spmd, body=%wide.region_1.4_spmd.sunk | while | flops 139200000 | bytes 3739867 | solution.py:97
  100.0 10.8 %while.117 = (s32[]{:T(128)}, f32[512,128]{1,0:T(8,128)S(1)}, f32[3072,128]{1,0:T(8,128)}, f32[3072,128]{1,0:T(8,128)S(1)}, s32[]{:T(128)}, /*index=5*/s32[512]{...) while((s32[]{:T(128)}, f32[512,128]{1,0:T(8,128)S(1)}, ...), condition=%wide.region_7.7_spmd, body=%wide.region_6.6_spmd.sunk | while | flops 338886656 | bytes 7229687 | solution.py:132
  116.1 5.4 %while.117 = (s32[]{:T(128)}, f32[512,128]{1,0:T(8,128)S(1)}, f32[3072,128]{1,0:T(8,128)}, f32[3072,128]{1,0:T(8,128)S(1)}, s32[]{:T(128)}, /*index=5*/s32[512]{...) while((s32[]{:T(128)}, f32[512,128]{1,0:T(8,128)S(1)}, ...), condition=%wide.region_7.7_spmd, body=%wide.region_6.6_spmd.sunk | while | flops 338886656 | bytes 7229687 | solution.py:132
  124.6 4.5 %while.116 = (s32[]{:T(128)}, f32[512]{0:T(512)S(1)}, f32[512]{0:T(512)S(1)}, f32[512]{0:T(512)S(1)}, s32[]{:T(128)}, /*index=5*/s32[512]{0:T(512)S(1)}, s32[307...) while((s32[]{:T(128)}, f32[512]{0:T(512)S(1)}, ...), condition=%wide.region_5.5_spmd, body=%wide.region_1.4_spmd.sunk | while | flops 139200000 | bytes 3739867 | solution.py:97
  129.2 10.8 %while.117 = (s32[]{:T(128)}, f32[512,128]{1,0:T(8,128)S(1)}, f32[3072,128]{1,0:T(8,128)}, f32[3072,128]{1,0:T(8,128)S(1)}, s32[]{:T(128)}, /*index=5*/s32[512]{...) while((s32[]{:T(128)}, f32[512,128]{1,0:T(8,128)S(1)}, ...), condition=%wide.region_7.7_spmd, body=%wide.region_6.6_spmd.sunk | while | flops 338886656 | bytes 7229687 | solution.py:132
  140.7 4.2 %all-to-all-start.4 = ((bf16[16,128,128]{2,1,0:T(8,128)(2,1)}), bf16[16,128,128]{2,1,0:T(8,128)(2,1)S(1)}, u32[]{:S(2)}, u32[]{:S(2)}) async-start(bf16[16,128,128]{2,1,0:T(8,128)(2,1)} %bitcast.142), calls=%async_computation.4 | async-start | bytes 1048576 | tf_op jit(solution)/shard_map/all_to_all | solution.py:159
  146.3 22.9 %collective-permute-done.3 = bf16[896,128]{1,0:T(8,128)(2,1)S(1)} collective-permute-done((bf16[896,128]{1,0:T(8,128)(2,1)S(1)}, bf16[896,128]{1,0:T(8,128)(2,1)S(1)}, u32[]{:S(2)}, u32[]{:S(2)}) %collective-permute-start.3) | collective-permute-done | bytes 229408 | tf_op jit(solution)/shard_map/ppermute | solution.py:14
  170.1 5.7 %all-to-all-start.6 = ((bf16[16,128,128]{2,1,0:T(8,128)(2,1)}), bf16[16,128,128]{2,1,0:T(8,128)(2,1)S(1)}, u32[]{:S(2)}, u32[]{:S(2)}) async-start(bf16[16,128,128]{2,1,0:T(8,128)(2,1)} %bitcast.36), calls=%async_computation.6 | async-start | bytes 1048576 | tf_op jit(solution)/shard_map/all_to_all | solution.py:161
  178.6 10.4 %collective-permute-done.2 = bf16[896,128]{1,0:T(8,128)(2,1)S(1)} collective-permute-done((bf16[896,128]{1,0:T(8,128)(2,1)S(1)}, bf16[896,128]{1,0:T(8,128)(2,1)S(1)}, u32[]{:S(2)}, u32[]{:S(2)}) %collective-permute-start.2) | collective-permute-done | bytes 229408 | tf_op jit(solution)/shard_map/ppermute | solution.py:14
  190.9 5.7 %all-to-all-start.5 = ((bf16[16,128,128]{2,1,0:T(8,128)(2,1)}), bf16[16,128,128]{2,1,0:T(8,128)(2,1)S(1)}, u32[]{:S(2)}, u32[]{:S(2)}) async-start(bf16[16,128,128]{2,1,0:T(8,128)(2,1)} %bitcast.33), calls=%async_computation.5 | async-start | bytes 1048576 | tf_op jit(solution)/shard_map/all_to_all | solution.py:160
  199.2 11.7 %all-to-all-done.5 = bf16[16,128,128]{2,1,0:T(8,128)(2,1)S(1)} async-done(((bf16[16,128,128]{2,1,0:T(8,128)(2,1)}), bf16[16,128,128]{2,1,0:T(8,128)(2,1)S(1)}, u32[]{:S(2)}, u32[]{:S(2)}) %all-to-all-start.5) | async-done | bytes 524320 | tf_op jit(solution)/shard_map/all_to_all | solution.py:160
  (204 shorter events, 85.9 us)
Async XLA Ops:
  0.6 1.0 copy-start
  0.6 9.5 %copy-start.2 = (bf16[128,2048]{1,0:T(8,128)(2,1)S(1)}, bf16[128,2048]{1,0:T(8,128)(2,1)}, u32[]{:S(2)}) copy-start(bf16[128,2048]{1,0:T(8,128)(2,1)} %param.12) | copy-start | bytes 1572868
  2.6 26.0 %copy-start.3 = (bf16[128,2048]{1,0:T(8,128)(2,1)S(1)}, bf16[128,2048]{1,0:T(8,128)(2,1)}, u32[]{:S(2)}) copy-start(bf16[128,2048]{1,0:T(8,128)(2,1)} %param.11) | copy-start | bytes 1572868
  2.6 21.8 %all-to-all-start.3 = ((bf16[128,16,128]{2,0,1:T(8,128)(2,1)}), bf16[128,16,128]{2,0,1:T(8,128)(2,1)S(1)}, u32[]{:S(2)}, u32[]{:S(2)}) async-start(bf16[128,16,128]{2,0,1:T(8,128)(2,1)} %copy_bitcast_fusion), calls=%async_computation.3 | async-start | bytes 1048576 | tf_op jit(solution)/shard_map/all_to_all | solution.py:24
  20.1 26.9 %copy-start.4 = (bf16[128,2048]{1,0:T(8,128)(2,1)S(1)}, bf16[128,2048]{1,0:T(8,128)(2,1)}, u32[]{:S(2)}) copy-start(bf16[128,2048]{1,0:T(8,128)(2,1)} %param.14) | copy-start | bytes 1572868
  24.4 18.4 %all-to-all-start.2 = ((bf16[16,128,128]{2,1,0:T(8,128)(2,1)}), bf16[16,128,128]{2,1,0:T(8,128)(2,1)S(1)}, u32[]{:S(2)}, u32[]{:S(2)}) async-start(bf16[16,128,128]{2,1,0:T(8,128)(2,1)} %constant_dynamic-update-slice_fusion), calls=%async_computation.2 | async-start | bytes 1048576 | tf_op jit(solution)/shard_map/all_to_all | solution.py:21
  42.8 18.4 %all-to-all-start = ((bf16[128,16,128]{2,0,1:T(8,128)(2,1)}), bf16[128,16,128]{2,0,1:T(8,128)(2,1)S(1)}, u32[]{:S(2)}, u32[]{:S(2)}) async-start(bf16[128,16,128]{2,0,1:T(8,128)(2,1)} %copy_bitcast_fusion.2), calls=%async_computation | async-start | bytes 1048576 | tf_op jit(solution)/shard_map/all_to_all | solution.py:19
  47.0 18.5 %copy-start.5 = (s32[32]{0:T(128)S(1)}, s32[32]{0:T(128)}, u32[]{:S(2)}) copy-start(s32[32]{0:T(128)} %param.15) | copy-start | bytes 388
  48.0 17.8 %collective-permute-start.1 = (bf16[896,128]{1,0:T(8,128)(2,1)S(1)}, bf16[896,128]{1,0:T(8,128)(2,1)S(1)}, u32[]{:S(2)}, u32[]{:S(2)}) collective-permute-start(bf16[896,128]{1,0:T(8,128)(2,1)S(1)} %bitcast.146), channel_id=1, source_target_pairs={{0,16},{1,17},{2,18},{3,19},{4,20},{5,21},{6,22},{7,23},{8,24},{9,... | collective-permute-start | bytes 688136 | tf_op jit(solution)/shard_map/ppermute | solution.py:14
  51.5 14.3 %collective-permute-start = (bf16[896,128]{1,0:T(8,128)(2,1)S(1)}, bf16[896,128]{1,0:T(8,128)(2,1)S(1)}, u32[]{:S(2)}, u32[]{:S(2)}) collective-permute-start(bf16[896,128]{1,0:T(8,128)(2,1)S(1)} %bitcast.147), channel_id=1, source_target_pairs={{0,16},{1,17},{2,18},{3,19},{4,20},{5,21},{6,22},{7,23},{8,24},{9,... | collective-permute-start | bytes 688136 | tf_op jit(solution)/shard_map/ppermute | solution.py:14
  61.3 8.8 %copy-start.1 = (bf16[128,16,128]{2,0,1:T(8,128)(2,1)}, bf16[128,16,128]{2,0,1:T(8,128)(2,1)S(1)}, u32[]{:S(2)}) copy-start(bf16[128,16,128]{2,0,1:T(8,128)(2,1)S(1)} %all-to-all-done) | copy-start | bytes 1572868
  61.3 18.5 %all-to-all-start.1 = ((bf16[128,16,128]{2,0,1:T(8,128)(2,1)}), bf16[128,16,128]{2,0,1:T(8,128)(2,1)}, u32[]{:S(2)}, u32[]{:S(2)}) async-start(bf16[128,16,128]{2,0,1:T(8,128)(2,1)} %copy_bitcast_fusion.1), calls=%async_computation.1 | async-start | bytes 1048576 | tf_op jit(solution)/shard_map/all_to_all | solution.py:25
  140.7 29.4 %all-to-all-start.4 = ((bf16[16,128,128]{2,1,0:T(8,128)(2,1)}), bf16[16,128,128]{2,1,0:T(8,128)(2,1)S(1)}, u32[]{:S(2)}, u32[]{:S(2)}) async-start(bf16[16,128,128]{2,1,0:T(8,128)(2,1)} %bitcast.142), calls=%async_computation.4 | async-start | bytes 1048576 | tf_op jit(solution)/shard_map/all_to_all | solution.py:159
  144.9 24.2 %collective-permute-start.3 = (bf16[896,128]{1,0:T(8,128)(2,1)S(1)}, bf16[896,128]{1,0:T(8,128)(2,1)S(1)}, u32[]{:S(2)}, u32[]{:S(2)}) collective-permute-start(bf16[896,128]{1,0:T(8,128)(2,1)S(1)} %slice.80), channel_id=1, source_target_pairs={{16,0},{17,1},{18,2},{19,3},{20,4},{21,5},{22,6},{23,7},{24,8},{25... | collective-permute-start | bytes 688136 | tf_op jit(solution)/shard_map/ppermute | solution.py:14
  170.1 20.9 %all-to-all-start.6 = ((bf16[16,128,128]{2,1,0:T(8,128)(2,1)}), bf16[16,128,128]{2,1,0:T(8,128)(2,1)S(1)}, u32[]{:S(2)}, u32[]{:S(2)}) async-start(bf16[16,128,128]{2,1,0:T(8,128)(2,1)} %bitcast.36), calls=%async_computation.6 | async-start | bytes 1048576 | tf_op jit(solution)/shard_map/all_to_all | solution.py:161
  177.3 11.7 %collective-permute-start.2 = (bf16[896,128]{1,0:T(8,128)(2,1)S(1)}, bf16[896,128]{1,0:T(8,128)(2,1)S(1)}, u32[]{:S(2)}, u32[]{:S(2)}) collective-permute-start(bf16[896,128]{1,0:T(8,128)(2,1)S(1)} %slice.78), channel_id=1, source_target_pairs={{16,0},{17,1},{18,2},{19,3},{20,4},{21,5},{22,6},{23,7},{24,8},{25... | collective-permute-start | bytes 688136 | tf_op jit(solution)/shard_map/ppermute | solution.py:14
  190.9 20.0 %all-to-all-start.5 = ((bf16[16,128,128]{2,1,0:T(8,128)(2,1)}), bf16[16,128,128]{2,1,0:T(8,128)(2,1)S(1)}, u32[]{:S(2)}, u32[]{:S(2)}) async-start(bf16[16,128,128]{2,1,0:T(8,128)(2,1)} %bitcast.33), calls=%async_computation.5 | async-start | bytes 1048576 | tf_op jit(solution)/shard_map/all_to_all | solution.py:160
